TPU v7x, 512 devices: a whole 4x8x8 slice. The times are simulated.
512 devices in a mesh: row: 16 (over y, core), col: 32 (over z, x).
Axes of the slice: x: 4, y: 8, z: 8, core: 2. Of those that a mesh axis runs over, the one named last changes fastest.
Arguments:
- row_points: bfloat16 [64, 4096], P(None, 'row'), may hold values from -6 to 6
- col_points: bfloat16 [64, 262144], P(None, 'col'), may hold values from -6 to 6
- random_panel: bfloat16 [262144, 128], P('col'), may hold values from -6 to 6
Outputs:
- left_basis: float32 [4096, 128], P('row')
- coefficients: bfloat16 [128, 262144], P('row', 'col')
All inputs are finite; a program needn't handle non-finite values.
Results may differ from a plain program's by a relative error of at most 0.015.
Values may be sent and summed in bfloat16 or wider, within the bound.
A program may use at most 64 MiB of HBM per device.

v0:
```python
import math
import jax
import jax.numpy as jnp
from jax import lax
from jax.sharding import PartitionSpec as P


def kernel_tile(points_left, left_sq, col_block, exp_scale):
    cross = jnp.einsum("kr,kc->rc", points_left, col_block, preferred_element_type=jnp.float32)
    col_sq = jnp.sum(jnp.square(col_block.astype(jnp.float32)), axis=0)
    return jnp.exp((2.0 * cross - left_sq[:, None] - col_sq[None, :]) * exp_scale)


def per_device(row_points, col_points, random_panel):
    feature_dim, row_dev = row_points.shape
    col_dev, sketch_width = random_panel.shape
    exp_scale = 2.0 / feature_dim
    row_sq = jnp.sum(jnp.square(row_points.astype(jnp.float32)), axis=0)
    block_width = math.gcd(col_dev, 2048)
    block_count = col_dev // block_width
    blocks = col_points.reshape(feature_dim, block_count, block_width).transpose(1, 0, 2)
    panel_blocks = random_panel.reshape(block_count, block_width, sketch_width)
    start_sum = jnp.zeros((row_dev, sketch_width), jnp.float32)

    def add_keep(accum_sum, block_pair):
        kernel = kernel_tile(row_points, row_sq, block_pair[0], exp_scale).astype(jnp.bfloat16)
        return (
            accum_sum + jnp.dot(kernel, block_pair[1], preferred_element_type=jnp.float32),
            kernel,
        )

    partial_value, kernels = lax.scan(add_keep, start_sum, (blocks, panel_blocks))
    sketch = lax.psum(partial_value, "col")
    local_gram = jnp.dot(
        sketch.T, sketch, precision=lax.Precision.HIGHEST, preferred_element_type=jnp.float32
    )
    gram_matrix = lax.psum(local_gram, "row")
    factor = jnp.linalg.cholesky(gram_matrix)
    orthonormal = jax.scipy.linalg.solve_triangular(factor, sketch.T, lower=True).T
    left_basis = orthonormal * math.sqrt(row_dev * lax.axis_size("row"))
    orth_bf = orthonormal.astype(jnp.bfloat16)
    all_terms = jnp.einsum("rq,nrc->qnc", orth_bf, kernels, preferred_element_type=jnp.float32)
    all_terms = all_terms.reshape(sketch_width, col_dev)
    coefficients = lax.psum_scatter(
        all_terms.astype(jnp.bfloat16), "row", scatter_dimension=0, tiled=True
    )
    return (left_basis, coefficients)


def solution(mesh):
    placed = (P(None, "row"), P(None, "col"), P("col", None))
    return jax.shard_map(
        per_device,
        mesh=mesh,
        in_specs=placed,
        out_specs=(P("row", None), P("row", "col")),
        check_vma=False,
    )
```

profile of v0, /device:TPU:25, one launch (start us, length us, event | category | flops | bytes accessed | tf_op | source)
XLA Modules:
  0.0 394.3 jit_solution(6189894932676397929)
XLA Ops:
  7.2 1.9 reshape.24
  9.7 13.3 %while.13 = (s32[]{:T(128)}, f32[256,128]{1,0:T(8,128)S(1)}, bf16[4,256,2048]{1,2,0:T(8,128)(2,1)}, bf16[4,64,2048]{2,1,0:T(8,128)(2,1)S(1)}, bf16[64,256]{1,0:T...) while((s32[]{:T(128)}, f32[256,128]{1,0:T(8,128)S(1)}, ...), condition=%wide.region_3.4_spmd.clone, body=%wide.region_1.3_spmd.clone.sunk | while | flops 204404736 | bytes 4508267 | solution.py:32
  9.8 1.7 bitcast_dynamic-update-slice_fusion.2
  11.5 1.5 convolution_add_fusion.2
  13.1 1.7 bitcast_dynamic-update-slice_fusion.2
  14.9 1.5 convolution_add_fusion.2
  16.5 1.7 bitcast_dynamic-update-slice_fusion.2
  18.2 1.5 convolution_add_fusion.2
  19.8 1.7 bitcast_dynamic-update-slice_fusion.2
  21.5 1.5 convolution_add_fusion.2
  23.1 0.6 copy-done
  23.8 154.0 %all-reduce.3.cloned.1.call-done = f32[256,128]{1,0:T(8,128)} async-done(((f32[256,128]{1,0:T(8,128)}), f32[256,128]{1,0:T(8,128)}) %all-reduce.3.cloned.1.call-update) | async-done | bytes 131088 | tf_op jit(solution)/shard_map/psum | solution.py:33
  177.8 2.0 fusion.17
  179.9 109.6 %all-reduce.5.cloned.1.call-done = f32[128,128]{0,1:T(8,128)} async-done(((f32[128,128]{0,1:T(8,128)}), f32[128,128]{0,1:T(8,128)}) %all-reduce.5.cloned.1.call-update) | async-done | bytes 65552 | tf_op jit(solution)/shard_map/psum | solution.py:37
  289.5 0.9 copy.18
  290.5 0.9 fusion.15
  291.3 11.7 %cholesky.16 = f32[128,128]{1,0:T(8,128)S(1)} custom-call(f32[128,128]{1,0:T(8,128)S(1)} %fusion.15), custom_call_target="Cholesky" | custom-call | tf_op jit(solution)/shard_map/jit(cholesky)/cholesky | solution.py:38
  303.7 0.7 fusion.11
  304.4 9.8 %custom-call.7 = f32[1,128,128]{1,2,0:T(8,128)S(1)} custom-call(f32[1,128,128]{2,1,0:T(8,128)S(1)} %fusion.11), custom_call_target="InvertDiagBlocksLowerTriangular" | custom-call | tf_op jit(solution)/shard_map/jit(_solve_triangular)/triangular_solve | solution.py:39
  314.2 1.8 broadcast_multiply_fusion
  316.0 3.7 convolution_convert_fusion
  319.7 2.5 copy.21
  322.2 4.1 %copy.27 = bf16[128,8192]{1,0:T(8,128)(2,1)} copy(bf16[128,8192]{0,1:T(8,128)(2,1)} %bitcast.49) | data formatting | bytes 4194304
  326.3 61.5 %reduce-scatter.4.cloned.1.call-done = bf16[8,8192]{1,0:T(8,128)(2,1)} async-done(((bf16[128,8192]{1,0:T(8,128)(2,1)}), bf16[8,8192]{1,0:T(8,128)(2,1)}) %reduce-scatter.4.cloned.1.call-update) | async-done | bytes 131088
  (19 shorter events, 1.8 us)
Async XLA Ops:
  7.2 170.7 %all-reduce.3.cloned.1.call-start = ((), (), s32[]{:S(2)}) async-start(), calls=%async_computation.1 | async-start | bytes 262144 | tf_op jit(solution)/shard_map/psum | solution.py:33
  7.2 2.5 copy-start.1
  23.1 0.7 copy-start
  23.7 265.8 %all-reduce.5.cloned.1.call-start = ((), (), s32[]{:S(2)}) async-start(), calls=%async_computation.2 | async-start | bytes 131072 | tf_op jit(solution)/shard_map/psum | solution.py:37
  179.8 208.0 %reduce-scatter.4.cloned.1.call-start = ((), (), s32[]{:S(2)}) async-start(), calls=%async_computation.3 | async-start | bytes 2228224
Sparse Core Ops, SparseCore 0:
  23.9 153.9 all-reduce.2
  180.7 108.7 all-reduce.4
  326.5 61.2 reduce-scatter.3
where the time goes:
time: 395 us; the launch traced here: 394 us
  waiting for transfers between devices  325 us (82%)
  other arithmetic  24 us (6%)
  matrix products  20.4 us (5%)
  between operations  13.8 us (3%)
  local copies, waits for them, and re-layouts  10.6 us (3%)
    psum x1, waiting for transfers between devices, per_device(): sketch = lax.psum(partial_value, 'col')  154 us
    psum x1, waiting for transfers between devices, per_device(): gram_matrix = lax.psum(local_gram, 'row')  110 us
    unnamed x4, waiting for transfers between devices  61.5 us
    another operation x3, other arithmetic, per_device(): factor = jnp.linalg.cholesky(gram_matrix)  12.4 us
    another operation x2, other arithmetic, per_device(): jax.scipy.linalg.solve_triangular(factor, sketch.T, lower=True)  10.5 us
  transfers between devices with their start and end apart: 3, of which 3 were waited for; matrix products, arithmetic and copies ran while one was open for 0% of the time, Pallas kernels for 0%

commit v1 on v0

--- a/solution.py
+++ b/solution.py
@@ -30,7 +30,7 @@
         )
 
     partial_value, kernels = lax.scan(add_keep, start_sum, (blocks, panel_blocks))
-    sketch = lax.psum(partial_value, "col")
+    sketch = jnp.sum(lax.all_gather(partial_value, "col"), axis=0)
     local_gram = jnp.dot(
         sketch.T, sketch, precision=lax.Precision.HIGHEST, preferred_element_type=jnp.float32
     )

time: 395 us -> 327 us (0.83)
  waiting for transfers between devices: 325 us -> 257 us
    psum x1 -> x0, waiting for transfers between devices: 154 us -> none  [per_device(): sketch = lax.psum(partial_value, 'col')]
    all_gather x0 -> x1, waiting for transfers between devices: none -> 88.8 us  [per_device(): sketch = jnp.sum(lax.all_gather(partial_value, 'col'), axis=0)]
where the time goes in v1:
time: 327 us; the launch traced here: 326 us
  waiting for transfers between devices  257 us (79%)
  other arithmetic  26.4 us (8%)
  matrix products  18.5 us (6%)
  between operations  13.8 us (4%)
  local copies, waits for them, and re-layouts  10.6 us (3%)
    psum x1, waiting for transfers between devices, per_device(): gram_matrix = lax.psum(local_gram, 'row')  106 us
    all_gather x1, waiting for transfers between devices, per_device(): sketch = jnp.sum(lax.all_gather(partial_value, 'col'), axis=0)  88.8 us
    unnamed x4, waiting for transfers between devices  61.5 us
    another operation x3, other arithmetic, per_device(): factor = jnp.linalg.cholesky(gram_matrix)  12.4 us
    another operation x2, other arithmetic, per_device(): jax.scipy.linalg.solve_triangular(factor, sketch.T, lower=True)  10.5 us
    dot_general x4, matrix products, kernel_tile(): jnp.einsum('kr,kc->rc', points_left, col_block, preferred_element_type=jn...  6.73 us
  transfers between devices with their start and end apart: 3, of which 3 were waited for; matrix products, arithmetic and copies ran while one was open for 0% of the time, Pallas kernels for 0%

profile of v1, /device:TPU:25, one launch (start us, length us, event | category | flops | bytes accessed | tf_op | source)
XLA Modules:
  0.0 326.5 jit_solution(10240326586997574989)
XLA Ops:
  7.2 1.9 reshape.24
  9.7 13.3 %while.13 = (s32[]{:T(128)}, f32[256,128]{1,0:T(8,128)S(1)}, bf16[4,256,2048]{1,2,0:T(8,128)(2,1)}, bf16[4,64,2048]{2,1,0:T(8,128)(2,1)S(1)}, bf16[64,256]{1,0:T...) while((s32[]{:T(128)}, f32[256,128]{1,0:T(8,128)S(1)}, ...), condition=%wide.region_3.4_spmd.clone, body=%wide.region_1.3_spmd.clone.sunk | while | flops 204404736 | bytes 4508267 | solution.py:32
  9.8 1.7 bitcast_dynamic-update-slice_fusion.2
  11.5 1.5 convolution_add_fusion.2
  13.1 1.7 bitcast_dynamic-update-slice_fusion.2
  14.9 1.5 convolution_add_fusion.2
  16.5 1.7 bitcast_dynamic-update-slice_fusion.2
  18.2 1.5 convolution_add_fusion.2
  19.8 1.7 bitcast_dynamic-update-slice_fusion.2
  21.5 1.5 convolution_add_fusion.2
  23.8 88.8 %all-gather.3.cloned.1.call-done = f32[8192,128]{1,0:T(8,128)} async-done(((f32[256,128]{1,0:T(8,128)}), f32[8192,128]{1,0:T(8,128)}) %all-gather.3.cloned.1.call-update) | async-done | bytes 4194320 | tf_op jit(solution)/shard_map/all_gather | solution.py:33
  112.6 2.4 reduce_sum.28
  115.0 1.0 fusion.17
  116.1 106.5 %all-reduce.2.cloned.1.call-done = f32[128,128]{0,1:T(8,128)} async-done(((f32[128,128]{0,1:T(8,128)}), f32[128,128]{0,1:T(8,128)}) %all-reduce.2.cloned.1.call-update) | async-done | bytes 65552 | tf_op jit(solution)/shard_map/psum | solution.py:37
  222.6 0.9 copy.18
  223.5 0.9 fusion.15
  224.4 11.7 %cholesky.16 = f32[128,128]{1,0:T(8,128)S(1)} custom-call(f32[128,128]{1,0:T(8,128)S(1)} %fusion.15), custom_call_target="Cholesky" | custom-call | tf_op jit(solution)/shard_map/jit(cholesky)/cholesky | solution.py:38
  236.8 0.7 fusion.11
  237.4 9.8 %custom-call.7 = f32[1,128,128]{1,2,0:T(8,128)S(1)} custom-call(f32[1,128,128]{2,1,0:T(8,128)S(1)} %fusion.11), custom_call_target="InvertDiagBlocksLowerTriangular" | custom-call | tf_op jit(solution)/shard_map/jit(_solve_triangular)/triangular_solve | solution.py:39
  247.2 0.9 broadcast_multiply_fusion
  248.2 3.7 %convolution_convert_fusion = bf16[128,4,2048]{2,0,1:T(8,128)(2,1)S(1)} fusion(bf16[4,256,2048]{1,2,0:T(8,128)(2,1)} %get-tuple-element.41, bf16[256,128]{1,0:T(8,128)(2,1)S(1)} %get-tuple-element.101), kind=kOutput, calls=%fused_computation.15 | convolution fusion | flops 537919488 | bytes 6356992 | tf_op jit(solution)/shard_map/rq,nrc->qnc/dot_general | solution.py:42
  251.8 2.5 copy.21
  254.4 4.1 %copy.27 = bf16[128,8192]{1,0:T(8,128)(2,1)} copy(bf16[128,8192]{0,1:T(8,128)(2,1)} %bitcast.50) | data formatting | bytes 4194304
  258.5 61.5 %reduce-scatter.4.cloned.1.call-done = bf16[8,8192]{1,0:T(8,128)(2,1)} async-done(((bf16[128,8192]{1,0:T(8,128)(2,1)}), bf16[8,8192]{1,0:T(8,128)(2,1)}) %reduce-scatter.4.cloned.1.call-update) | async-done | bytes 131088
  (20 shorter events, 2.4 us)
Async XLA Ops:
  7.2 105.4 %all-gather.3.cloned.1.call-start = ((), (), s32[]{:S(2)}) async-start(), calls=%async_computation.2 | async-start | bytes 4325376 | tf_op jit(solution)/shard_map/all_gather | solution.py:33
  7.2 2.5 copy-start.1
  23.1 0.7 copy-start
  23.7 198.8 %all-reduce.2.cloned.1.call-start = ((), (), s32[]{:S(2)}) async-start(), calls=%async_computation.1 | async-start | bytes 131072 | tf_op jit(solution)/shard_map/psum | solution.py:37
  116.0 203.9 %reduce-scatter.4.cloned.1.call-start = ((), (), s32[]{:S(2)}) async-start(), calls=%async_computation.3 | async-start | bytes 2228224
Sparse Core Ops, SparseCore 0:
  23.9 88.7 all-gather.2
  116.2 106.3 all-reduce.1
  258.6 61.2 reduce-scatter.3
